TPU v7x, 32 devices: a whole 2x2x4 slice. The times are simulated.
32 devices in a mesh: seq: 8 (over z, x), vocab: 4 (over y, core).
Axes of the slice: x: 2, y: 2, z: 4, core: 2. Of those that a mesh axis runs over, the one named last changes fastest.
Arguments:
- rollout: bfloat16 [288, 4096], P('seq')
- group_count: int32 [8], replicated, may hold values from 12 to 36, as said below
- final_gain: float32 [4096], replicated, may hold values from 0.5 to 1.5
- head_weight: bfloat16 [4096, 152064], P(None, ('seq', 'vocab'))
- teacher_index: int32 [192, 64], replicated, may hold values from 0 to 152063, as said below
- teacher_logprob: float32 [192, 64], replicated, as said below
Outputs:
- kl: float32 [192], P('seq')
- grad_weight: bfloat16 [4096, 152064], P(None, ('seq', 'vocab'))
- grad_rollout: bfloat16 [288, 4096], P('seq', 'vocab')
Inputs may be any that keep to these rules, and one draw needn't show every extreme that they name: The first group_count[g] of the 36 slots of group g are live, the rest padding; the counts sum to 192. `teacher_index`: the 64 ids of one token are distinct. `teacher_logprob`: the exponentials of one token's entries sum to less than 1.
All inputs are finite; a program needn't handle non-finite values.
Results may differ from a plain program's by a relative error of at most 0.0075.
Values may be sent and summed in bfloat16 or wider, within the bound.
A program may use at most 128 MiB of HBM per device.

v0:
```python
import jax
import jax.numpy as jnp
from jax import lax
from jax.sharding import PartitionSpec as P

norm_eps = 1e-06
loss_scale = 16.0


def per_device(rollout, group_count, final_gain, head_weight, teacher_index, teacher_logprob):
    groups = lax.axis_size("seq")
    gen_slots, feature_width = rollout.shape
    tokens = teacher_index.shape[0]
    pack_rows = tokens // groups
    capacity = -(-gen_slots // groups)
    own_index = lax.axis_index("seq")
    offsets = jnp.cumsum(group_count) - group_count
    own_offset = offsets[own_index]
    own_count = group_count[own_index]
    row_ids = jnp.arange(capacity * groups, dtype=jnp.int32)
    padded = jnp.pad(rollout, ((0, capacity * groups - gen_slots), (0, 0)))
    padded = jnp.where((row_ids < own_count)[:, None], padded, jnp.zeros_like(padded))
    outgoing = jnp.roll(padded.reshape(capacity, groups, feature_width), own_offset, axis=1)
    arriving = lax.all_to_all(outgoing, "seq", split_axis=1, concat_axis=1, tiled=True)
    slot_ids = jnp.arange(capacity, dtype=jnp.int32)[:, None]
    row_in_group = slot_ids * groups + (own_index - offsets[None, :]) % groups
    is_live = row_in_group < group_count[None, :]
    position = jnp.where(is_live, (offsets[None, :] + row_in_group) // groups, pack_rows)
    packed = jnp.zeros((pack_rows, feature_width), rollout.dtype)
    packed = packed.at[position.reshape(-1)].set(arriving.reshape(-1, feature_width), mode="drop")
    values = packed.astype(jnp.float32)
    inv_rms = lax.rsqrt(jnp.mean(values * values, axis=1, keepdims=True) + norm_eps)
    normed = (values * inv_rms * final_gain).astype(jnp.bfloat16)
    all_rows = lax.all_gather(normed, "seq", axis=0, tiled=True)
    logits = jnp.dot(all_rows, head_weight, preferred_element_type=jnp.float32)
    vocab_dev = head_weight.shape[1]
    first_column = lax.axis_index(("seq", "vocab")) * vocab_dev
    local_index = teacher_index - first_column
    owned = (local_index >= 0) & (local_index < vocab_dev)
    teacher_prob = jnp.exp(teacher_logprob)
    teacher_mass = jnp.sum(teacher_prob, axis=1)
    token_ids = jnp.arange(tokens, dtype=jnp.int32)[:, None]
    column = jnp.where(owned, local_index, vocab_dev)
    teacher_dense = (
        jnp.zeros((tokens, vocab_dev), jnp.float32)
        .at[token_ids, column]
        .add(teacher_prob, mode="drop")
    )
    target_part = jnp.sum(teacher_dense * logits, axis=1)
    local_peak = jnp.max(logits, axis=1)
    row_peak = lax.pmax(local_peak, ("seq", "vocab"))
    local_total = jnp.sum(jnp.exp(logits - row_peak[:, None]), axis=1)
    row_total, target_sum = lax.psum((local_total, target_part), ("seq", "vocab"))
    log_total = row_peak + jnp.log(row_total)
    kl_all = jnp.sum(teacher_prob * teacher_logprob, axis=1) - target_sum + teacher_mass * log_total
    kl = lax.dynamic_slice_in_dim(kl_all, own_index * pack_rows, pack_rows)
    student_part = teacher_mass[:, None] * jnp.exp(logits - log_total[:, None]) - teacher_dense
    grad_logits = (loss_scale * student_part).astype(jnp.bfloat16)
    grad_weight = lax.dot_general(
        all_rows, grad_logits, (((0,), (0,)), ((), ())), preferred_element_type=jnp.float32
    ).astype(jnp.bfloat16)
    share = feature_width // lax.axis_size("vocab")
    feature_start = lax.axis_index("vocab") * share
    x_share = lax.dynamic_slice_in_dim(values, feature_start, share, 1)
    partial_rows = lax.psum_scatter(
        lax.dot_general(
            grad_logits, head_weight, (((1,), (1,)), ((), ())), preferred_element_type=jnp.float32
        ),
        "seq",
        scatter_dimension=0,
        tiled=True,
    )
    whole_rows = lax.psum(partial_rows, "vocab")
    full_grad = whole_rows * final_gain
    row_dots = jnp.sum(full_grad * values, axis=1, keepdims=True)
    scaled_grad = lax.dynamic_slice_in_dim(full_grad, feature_start, share, 1)
    grad_packed = (
        (scaled_grad - x_share * inv_rms * inv_rms * row_dots / feature_width) * inv_rms
    ).astype(jnp.bfloat16)
    taken = jnp.take(grad_packed, jnp.minimum(position, pack_rows - 1), axis=0)
    outgoing_back = jnp.where(is_live[:, :, None], taken, jnp.zeros_like(taken))
    coming_back = lax.all_to_all(outgoing_back, "seq", split_axis=1, concat_axis=1, tiled=True)
    restored = jnp.roll(coming_back, -own_offset, axis=1).reshape(capacity * groups, share)
    grad_rollout = restored[:gen_slots]
    return (kl, grad_weight, grad_rollout)


def solution(mesh):
    placed = (P("seq", None), P(), P(), P(None, ("seq", "vocab")), P(), P())
    return jax.shard_map(
        per_device,
        mesh=mesh,
        in_specs=placed,
        out_specs=(P("seq"), P(None, ("seq", "vocab")), P("seq", "vocab")),
        check_vma=False,
    )
```

profile of v0, /device:TPU:0, one launch (start us, length us, event | category | flops | bytes accessed | tf_op | source)
XLA Modules:
  0.0 382.8 jit_solution(6932193462676987082)
XLA Ops:
  7.2 1.3 dynamic_slice.23
  8.5 0.8 reduce-window.9
  9.3 0.7 and_select_fusion.1
  10.0 0.6 dynamic_slice.24
  12.5 0.7 iota_compare_fusion
  13.2 1.1 select_bitcast_fusion
  14.3 0.2 fusion.2
  14.6 1.0 copy.18
  15.5 7.3 %all-to-all-start = ((bf16[5,8,4096]{2,0,1:T(8,128)(2,1)}), bf16[5,8,4096]{2,0,1:T(8,128)(2,1)S(1)}, u32[]{:S(2)}, u32[]{:S(2)}) async-start(bf16[5,8,4096]{2,0,1:T(8,128)(2,1)} %copy.18), calls=%async_computation | async-start | bytes 1048576 | tf_op jit(solution)/shard_map/all_to_all | solution.py:24
  22.9 0.7 compare_and_fusion
  23.9 13.4 %all-to-all-done = bf16[5,8,4096]{2,0,1:T(8,128)(2,1)S(1)} async-done(((bf16[5,8,4096]{2,0,1:T(8,128)(2,1)}), bf16[5,8,4096]{2,0,1:T(8,128)(2,1)S(1)}, u32[]{:S(2)}, u32[]{:S(2)}) %all-to-all-start) | async-done | bytes 327712 | tf_op jit(solution)/shard_map/all_to_all | solution.py:24
  37.3 1.4 scatter_custom_fusion
  38.7 0.2 multiply_reduce_fusion.2
  38.9 0.8 multiply_convert_fusion.1
  39.9 0.1 and_reduce_fusion
  40.5 66.5 %scatter_custom_fusion.1 = f32[912384]{0:T(1024)} fusion(s32[12288]{0:T(1024)S(1)} %reshape.401, f32[12288]{0:T(1024)S(1)} %reshape.403, f32[]{:T(128)} %constant.100.clone.1), kind=kCustom, calls=%fused_computation.7 | custom fusion | flops 12288 | bytes 3649540
  107.0 5.8 %reshape.384 = f32[192,4752]{1,0:T(8,128)} reshape(f32[912384]{0:T(1024)} %scatter_custom_fusion.1) | data formatting | bytes 7299072 | tf_op jit(solution)/shard_map/scatter-add | solution.py:47
  112.7 20.6 %fusion.31 = (f32[192]{0:T(256)S(1)}, f32[192,4752]{1,0:T(8,128)}) fusion(bf16[192,4096]{1,0:T(8,128)(2,1)} %all-gather.2.cloned.1.call-done, bf16[4096,4752]{0,1:T(8,128)(2,1)} %param.9), kind=kOutput, calls=%fused_computation.86 | convolution fusion | flops 7475162112 | bytes 44151552 | tf_op jit(solution)/shard_map/dot_general | solution.py:35
  133.3 38.4 %pmax.7 = f32[192]{0:T(256)S(1)} all-reduce(f32[192]{0:T(256)S(1)} %get-tuple-element.18), channel_id=1, replica_groups=mesh['seq'=8,'vocab'=4] {'seq','vocab'}, use_global_device_ids=true, to_apply=%region_9.10 | all-reduce | flops 192 | bytes 1536 | tf_op jit(solution)/shard_map/pmax | solution.py:51
  171.7 4.2 %multiply_reduce_fusion = (f32[192]{0:T(256)S(1)}, f32[192]{0:T(256)S(1)}) fusion(f32[192,4752]{1,0:T(8,128)} %reshape.384, f32[192,4752]{1,0:T(8,128)} %get-tuple-element.19, f32[192]{0:T(256)S(1)} %pmax.7), kind=kLoop, calls=%fused_computation.6 | loop fusion | flops 3649152 | bytes 7301376 | tf_op jit(solution)/shard_map/reduce_sum | solution.py:49
  175.9 40.9 %all-reduce.1 = (f32[192]{0:T(256)S(1)}, f32[192]{0:T(256)S(1)}) all-reduce(f32[192]{0:T(256)S(1)} %get-tuple-element.4, f32[192]{0:T(256)S(1)} %get-tuple-element.3), channel_id=1, replica_groups=mesh['seq'=8,'vocab'=4] {'seq','vocab'}, use_global_device_ids=true, to_apply=%region_11.12 | all-reduce | flops 384 | bytes 3072 | tf_op jit(solution)/shard_map/psum | solution.py:53
  216.8 4.1 %multiply_convert_fusion = bf16[192,4752]{1,0:T(8,128)(2,1)S(1)} fusion(f32[192,4752]{1,0:T(8,128)} %reshape.384, f32[192,4752]{1,0:T(8,128)} %get-tuple-element.19, f32[192]{0:T(256)S(1)} %get-tuple-element.12, f32[192]{0:T(256)S(1)} %get-tuple-element.6), kind=kLoop, calls=%fused_computation.4 | loop fusion | flops 4561920 | bytes 9125376 | tf_op jit(solution)/shard_map/convert_element_type | solution.py:58
  220.9 18.2 %fusion.32 = f32[192,4096]{1,0:T(8,128)} fusion(bf16[192,4752]{1,0:T(8,128)(2,1)S(1)} %multiply_convert_fusion, bf16[4096,4752]{0,1:T(8,128)(2,1)} %param.9), kind=kOutput, calls=%fused_computation.87 | convolution fusion | flops 7474249728 | bytes 43898880 | tf_op jit(solution)/shard_map/dot_general | solution.py:66
  239.3 74.6 %reduce-scatter.2.cloned.1.call-done = f32[24,4096]{1,0:T(8,128)} async-done(((f32[192,4096]{1,0:T(8,128)}), f32[24,4096]{1,0:T(8,128)}) %reduce-scatter.2.cloned.1.call-update) | async-done | bytes 393232 | tf_op jit(solution)/shard_map/reduce_scatter | solution.py:65
  315.0 33.2 %all-reduce.4.cloned.1.call-done = f32[24,4096]{1,0:T(8,128)} async-done(((f32[24,4096]{1,0:T(8,128)}), f32[24,4096]{1,0:T(8,128)}) %all-reduce.4.cloned.1.call-update) | async-done | bytes 393232 | tf_op jit(solution)/shard_map/psum | solution.py:73
  348.2 1.2 multiply_reduce_fusion.1
  349.4 0.7 gather_fusion
  350.1 0.7 fusion.6
  350.8 5.5 %all-to-all-start.1 = ((bf16[5,8,1024]{2,0,1:T(8,128)(2,1)}), bf16[5,8,1024]{2,0,1:T(8,128)(2,1)S(1)}, u32[]{:S(2)}, u32[]{:S(2)}) async-start(bf16[5,8,1024]{2,0,1:T(8,128)(2,1)} %fusion.6), calls=%async_computation.2 | async-start | bytes 262144 | tf_op jit(solution)/shard_map/all_to_all | solution.py:82
  356.3 18.6 %convolution_convert_fusion = bf16[4096,4752]{0,1:T(8,128)(2,1)} fusion(bf16[192,4096]{1,0:T(8,128)(2,1)} %all-gather.2.cloned.1.call-done, bf16[192,4752]{1,0:T(8,128)(2,1)S(1)} %multiply_convert_fusion), kind=kOutput, calls=%fused_computation.3 | convolution fusion | flops 7493713920 | bytes 42326016 | tf_op jit(solution)/shard_map/dot_general | solution.py:59
  374.9 0.6 dynamic_slice.26
  375.6 0.7 fusion.9
  (44 shorter events, 1.5 us)
Async XLA Ops:
  7.2 32.7 %copy-start.5 = (s32[2]{0:T(128)S(1)}, s32[2]{0:T(128)}, u32[]{:S(2)}) copy-start(s32[2]{0:T(128)} %constant.127) | copy-start | bytes 28
  7.2 32.8 %copy-start.4 = (s32[2]{0:T(128)S(1)}, s32[2]{0:T(128)}, u32[]{:S(2)}) copy-start(s32[2]{0:T(128)} %constant.130) | copy-start | bytes 28
  7.2 31.7 %copy-start = (f32[4096]{0:T(1024)S(1)}, f32[4096]{0:T(1024)}, u32[]{:S(2)}) copy-start(f32[4096]{0:T(1024)} %param.8) | copy-start | bytes 49156
  7.2 32.6 %copy-start.1 = (s32[192,64]{0,1:T(8,128)S(1)}, s32[192,64]{0,1:T(8,128)}, u32[]{:S(2)}) copy-start(s32[192,64]{0,1:T(8,128)} %param.10) | copy-start | bytes 147460
  7.2 33.0 %copy-start.2 = (f32[192,64]{0,1:T(8,128)S(1)}, f32[192,64]{0,1:T(8,128)}, u32[]{:S(2)}) copy-start(f32[192,64]{0,1:T(8,128)} %param.11) | copy-start | bytes 147460
  15.5 21.8 %all-to-all-start = ((bf16[5,8,4096]{2,0,1:T(8,128)(2,1)}), bf16[5,8,4096]{2,0,1:T(8,128)(2,1)S(1)}, u32[]{:S(2)}, u32[]{:S(2)}) async-start(bf16[5,8,4096]{2,0,1:T(8,128)(2,1)} %copy.18), calls=%async_computation | async-start | bytes 1048576 | tf_op jit(solution)/shard_map/all_to_all | solution.py:24
  22.8 89.9 %all-gather.2.cloned.1.call-start = ((), (), s32[]{:S(2)}) async-start(), calls=%async_computation.3 | async-start | bytes 1769472 | tf_op jit(solution)/shard_map/all_gather | solution.py:34
  39.7 274.2 %reduce-scatter.2.cloned.1.call-start = ((), (), s32[]{:S(2)}) async-start(), calls=%async_computation.4 | async-start | bytes 3538944 | tf_op jit(solution)/shard_map/reduce_scatter | solution.py:65
  220.9 93.0 %copy-start.3 = (s32[8]{0:T(128)S(1)}, s32[8]{0:T(128)}, u32[]{:S(2)}) copy-start(s32[8]{0:T(128)} %param.7) | copy-start | bytes 100
  239.2 109.0 %all-reduce.4.cloned.1.call-start = ((), (), s32[]{:S(2)}) async-start(), calls=%async_computation.5 | async-start | bytes 786432 | tf_op jit(solution)/shard_map/psum | solution.py:73
  350.8 24.7 %all-to-all-start.1 = ((bf16[5,8,1024]{2,0,1:T(8,128)(2,1)}), bf16[5,8,1024]{2,0,1:T(8,128)(2,1)S(1)}, u32[]{:S(2)}, u32[]{:S(2)}) async-start(bf16[5,8,1024]{2,0,1:T(8,128)(2,1)} %fusion.6), calls=%async_computation.2 | async-start | bytes 262144 | tf_op jit(solution)/shard_map/all_to_all | solution.py:82
Sparse Core Ops, SparseCore 0:
  39.8 43.2 all-gather.1
  239.3 74.4 reduce-scatter.1
  316.2 31.8 all-reduce.3
where the time goes:
time: 384 us; the launch traced here: 383 us
  waiting for transfers between devices  121 us (32%)
  other arithmetic  83.2 us (22%)
  blocking collectives  79.3 us (21%)
  matrix products  57.5 us (15%)
  between operations  16.6 us (4%)
  starting transfers between devices  12.9 us (3%)
  local copies, waits for them, and re-layouts  12.1 us (3%)
    reduce_scatter x1, waiting for transfers between devices, per_device(): lax.psum_scatter(lax.dot_general(grad_logits, head_weight, (((1,), (1,)),...  74.6 us
    unnamed x4, other arithmetic  66.7 us
    psum x1, blocking collectives, per_device(): lax.psum((local_total, target_part), ('seq', 'vocab'))  40.9 us
    pmax x1, blocking collectives, per_device(): row_peak = lax.pmax(local_peak, ('seq', 'vocab'))  38.4 us
    psum x1, waiting for transfers between devices, per_device(): whole_rows = lax.psum(partial_rows, 'vocab')  33.2 us
    dot_general x1, matrix products, per_device(): logits = jnp.dot(all_rows, head_weight, preferred_element_type=jnp.float32)  20.6 us
    dot_general x1, matrix products, per_device(): lax.dot_general(all_rows, grad_logits, (((0,), (0,)), ((), ())), preferre...  18.6 us
    dot_general x1, matrix products, per_device(): lax.dot_general(grad_logits, head_weight, (((1,), (1,)), ((), ())), prefe...  18.2 us
  transfers between devices with their start and end apart: 5, of which 3 were waited for; matrix products, arithmetic and copies ran while one was open for 24% of the time, Pallas kernels for 0%

commit v1 on v0

--- a/solution.py
+++ b/solution.py
@@ -5,6 +5,11 @@
 
 norm_eps = 1e-06
 loss_scale = 16.0
+
+
+def derive_loops(local_x, net_axis):
+    after = lax.all_gather(local_x, net_axis)
+    return jnp.sum(after, 0)
 
 
 def per_device(rollout, group_count, final_gain, head_weight, teacher_index, teacher_logprob):
@@ -70,7 +75,7 @@
         scatter_dimension=0,
         tiled=True,
     )
-    whole_rows = lax.psum(partial_rows, "vocab")
+    whole_rows = derive_loops(partial_rows, "vocab")
     full_grad = whole_rows * final_gain
     row_dots = jnp.sum(full_grad * values, axis=1, keepdims=True)
     scaled_grad = lax.dynamic_slice_in_dim(full_grad, feature_start, share, 1)

time: 384 us -> 370 us (0.964)
  waiting for transfers between devices: 121 us -> 107 us
    psum x1 -> x0, waiting for transfers between devices: 33.2 us -> none  [per_device(): whole_rows = lax.psum(partial_rows, 'vocab')]
    all_gather x0 -> x1, waiting for transfers between devices: none -> 19.2 us  [derive_loops(): after = lax.all_gather(local_x, net_axis)]
  transfers between devices with their start and end apart: 5 -> 5, of which waited for: 3 -> 3; matrix products, arithmetic and copies ran while one was open for 24% -> 25% of each run, Pallas kernels for 0% -> 0%
where the time goes in v1:
time: 370 us; the launch traced here: 369 us
  waiting for transfers between devices  107 us (29%)
  other arithmetic  83.7 us (23%)
  blocking collectives  79.3 us (21%)
  matrix products  57.5 us (16%)
  between operations  16.6 us (4%)
  starting transfers between devices  12.9 us (3%)
  local copies, waits for them, and re-layouts  12.1 us (3%)
    reduce_scatter x1, waiting for transfers between devices, per_device(): lax.psum_scatter(lax.dot_general(grad_logits, head_weight, (((1,), (1,)),...  74.6 us
    unnamed x4, other arithmetic  66.7 us
    psum x1, blocking collectives, per_device(): lax.psum((local_total, target_part), ('seq', 'vocab'))  40.9 us
    pmax x1, blocking collectives, per_device(): row_peak = lax.pmax(local_peak, ('seq', 'vocab'))  38.4 us
    dot_general x1, matrix products, per_device(): logits = jnp.dot(all_rows, head_weight, preferred_element_type=jnp.float32)  20.6 us
    all_gather x1, waiting for transfers between devices, derive_loops(): after = lax.all_gather(local_x, net_axis)  19.2 us
    dot_general x1, matrix products, per_device(): lax.dot_general(all_rows, grad_logits, (((0,), (0,)), ((), ())), preferre...  18.6 us
    dot_general x1, matrix products, per_device(): lax.dot_general(grad_logits, head_weight, (((1,), (1,)), ((), ())), prefe...  18.2 us
  transfers between devices with their start and end apart: 5, of which 3 were waited for; matrix products, arithmetic and copies ran while one was open for 25% of the time, Pallas kernels for 0%

profile of v1, /device:TPU:0, one launch (start us, length us, event | category | flops | bytes accessed | tf_op | source)
XLA Modules:
  0.0 369.4 jit_solution(4648988111076316867)
XLA Ops:
  7.2 1.3 dynamic_slice.23
  8.5 0.8 reduce-window.9
  9.3 0.7 and_select_fusion.1
  10.0 0.6 dynamic_slice.24
  12.5 0.7 iota_compare_fusion
  13.2 1.1 select_bitcast_fusion
  14.3 0.2 fusion.2
  14.6 1.0 copy.18
  15.5 7.3 %all-to-all-start = ((bf16[5,8,4096]{2,0,1:T(8,128)(2,1)}), bf16[5,8,4096]{2,0,1:T(8,128)(2,1)S(1)}, u32[]{:S(2)}, u32[]{:S(2)}) async-start(bf16[5,8,4096]{2,0,1:T(8,128)(2,1)} %copy.18), calls=%async_computation | async-start | bytes 1048576 | tf_op jit(solution)/shard_map/all_to_all | solution.py:29
  22.9 0.7 compare_and_fusion
  23.9 13.4 %all-to-all-done = bf16[5,8,4096]{2,0,1:T(8,128)(2,1)S(1)} async-done(((bf16[5,8,4096]{2,0,1:T(8,128)(2,1)}), bf16[5,8,4096]{2,0,1:T(8,128)(2,1)S(1)}, u32[]{:S(2)}, u32[]{:S(2)}) %all-to-all-start) | async-done | bytes 327712 | tf_op jit(solution)/shard_map/all_to_all | solution.py:29
  37.3 1.4 scatter_custom_fusion
  38.7 0.2 multiply_reduce_fusion.2
  38.9 0.8 multiply_convert_fusion.1
  40.5 66.5 %scatter_custom_fusion.1 = f32[912384]{0:T(1024)} fusion(s32[12288]{0:T(1024)S(1)} %reshape.401, f32[12288]{0:T(1024)S(1)} %reshape.403, f32[]{:T(128)} %constant.100.clone.1), kind=kCustom, calls=%fused_computation.7 | custom fusion | flops 12288 | bytes 3649540
  107.0 5.8 %reshape.384 = f32[192,4752]{1,0:T(8,128)} reshape(f32[912384]{0:T(1024)} %scatter_custom_fusion.1) | data formatting | bytes 7299072 | tf_op jit(solution)/shard_map/scatter-add | solution.py:52
  112.7 20.6 %fusion.31 = (f32[192]{0:T(256)S(1)}, f32[192,4752]{1,0:T(8,128)}) fusion(bf16[192,4096]{1,0:T(8,128)(2,1)} %all-gather.4.cloned.1.call-done, bf16[4096,4752]{0,1:T(8,128)(2,1)} %param.9), kind=kOutput, calls=%fused_computation.86 | convolution fusion | flops 7475162112 | bytes 44151552 | tf_op jit(solution)/shard_map/dot_general | solution.py:40
  133.3 38.4 %pmax.7 = f32[192]{0:T(256)S(1)} all-reduce(f32[192]{0:T(256)S(1)} %get-tuple-element.18), channel_id=1, replica_groups=mesh['seq'=8,'vocab'=4] {'seq','vocab'}, use_global_device_ids=true, to_apply=%region_9.10 | all-reduce | flops 192 | bytes 1536 | tf_op jit(solution)/shard_map/pmax | solution.py:56
  171.7 4.2 %multiply_reduce_fusion = (f32[192]{0:T(256)S(1)}, f32[192]{0:T(256)S(1)}) fusion(f32[192,4752]{1,0:T(8,128)} %reshape.384, f32[192,4752]{1,0:T(8,128)} %get-tuple-element.19, f32[192]{0:T(256)S(1)} %pmax.7), kind=kLoop, calls=%fused_computation.6 | loop fusion | flops 3649152 | bytes 7301376 | tf_op jit(solution)/shard_map/reduce_sum | solution.py:54
  175.9 40.9 %all-reduce.1 = (f32[192]{0:T(256)S(1)}, f32[192]{0:T(256)S(1)}) all-reduce(f32[192]{0:T(256)S(1)} %get-tuple-element.4, f32[192]{0:T(256)S(1)} %get-tuple-element.3), channel_id=1, replica_groups=mesh['seq'=8,'vocab'=4] {'seq','vocab'}, use_global_device_ids=true, to_apply=%region_11.12 | all-reduce | flops 384 | bytes 3072 | tf_op jit(solution)/shard_map/psum | solution.py:58
  216.8 4.1 %multiply_convert_fusion = bf16[192,4752]{1,0:T(8,128)(2,1)S(1)} fusion(f32[192,4752]{1,0:T(8,128)} %reshape.384, f32[192,4752]{1,0:T(8,128)} %get-tuple-element.19, f32[192]{0:T(256)S(1)} %get-tuple-element.12, f32[192]{0:T(256)S(1)} %get-tuple-element.6), kind=kLoop, calls=%fused_computation.4 | loop fusion | flops 4561920 | bytes 9125376 | tf_op jit(solution)/shard_map/convert_element_type | solution.py:63
  220.9 18.2 %fusion.32 = f32[192,4096]{1,0:T(8,128)} fusion(bf16[192,4752]{1,0:T(8,128)(2,1)S(1)} %multiply_convert_fusion, bf16[4096,4752]{0,1:T(8,128)(2,1)} %param.9), kind=kOutput, calls=%fused_computation.87 | convolution fusion | flops 7474249728 | bytes 43898880 | tf_op jit(solution)/shard_map/dot_general | solution.py:71
  239.3 74.6 %reduce-scatter.2.cloned.1.call-done = f32[24,4096]{1,0:T(8,128)} async-done(((f32[192,4096]{1,0:T(8,128)}), f32[24,4096]{1,0:T(8,128)}) %reduce-scatter.2.cloned.1.call-update) | async-done | bytes 393232 | tf_op jit(solution)/shard_map/reduce_scatter | solution.py:70
  315.0 19.2 %all-gather.6.cloned.1.call-done = f32[96,4096]{1,0:T(8,128)} async-done(((f32[24,4096]{1,0:T(8,128)}), f32[96,4096]{1,0:T(8,128)}) %all-gather.6.cloned.1.call-update) | async-done | bytes 1572880 | tf_op jit(solution)/shard_map/all_gather | solution.py:11
  334.2 1.5 reduce_sum.68
  335.7 0.2 multiply_reduce_fusion.1
  336.0 0.7 gather_fusion
  336.7 0.7 fusion.6
  337.4 5.5 %all-to-all-start.1 = ((bf16[5,8,1024]{2,0,1:T(8,128)(2,1)}), bf16[5,8,1024]{2,0,1:T(8,128)(2,1)S(1)}, u32[]{:S(2)}, u32[]{:S(2)}) async-start(bf16[5,8,1024]{2,0,1:T(8,128)(2,1)} %fusion.6), calls=%async_computation.2 | async-start | bytes 262144 | tf_op jit(solution)/shard_map/all_to_all | solution.py:87
  342.9 18.6 %convolution_convert_fusion = bf16[4096,4752]{0,1:T(8,128)(2,1)} fusion(bf16[192,4096]{1,0:T(8,128)(2,1)} %all-gather.4.cloned.1.call-done, bf16[192,4752]{1,0:T(8,128)(2,1)S(1)} %multiply_convert_fusion), kind=kOutput, calls=%fused_computation.3 | convolution fusion | flops 7493713920 | bytes 42326016 | tf_op jit(solution)/shard_map/dot_general | solution.py:64
  361.5 0.6 dynamic_slice.26
  362.2 0.7 fusion.9
  (45 shorter events, 1.6 us)
Async XLA Ops:
  7.2 32.7 %copy-start.5 = (s32[2]{0:T(128)S(1)}, s32[2]{0:T(128)}, u32[]{:S(2)}) copy-start(s32[2]{0:T(128)} %constant.127) | copy-start | bytes 28
  7.2 32.8 %copy-start.4 = (s32[2]{0:T(128)S(1)}, s32[2]{0:T(128)}, u32[]{:S(2)}) copy-start(s32[2]{0:T(128)} %constant.130) | copy-start | bytes 28
  7.2 31.7 %copy-start = (f32[4096]{0:T(1024)S(1)}, f32[4096]{0:T(1024)}, u32[]{:S(2)}) copy-start(f32[4096]{0:T(1024)} %param.8) | copy-start | bytes 49156
  7.2 32.6 %copy-start.1 = (s32[192,64]{0,1:T(8,128)S(1)}, s32[192,64]{0,1:T(8,128)}, u32[]{:S(2)}) copy-start(s32[192,64]{0,1:T(8,128)} %param.10) | copy-start | bytes 147460
  7.2 33.0 %copy-start.2 = (f32[192,64]{0,1:T(8,128)S(1)}, f32[192,64]{0,1:T(8,128)}, u32[]{:S(2)}) copy-start(f32[192,64]{0,1:T(8,128)} %param.11) | copy-start | bytes 147460
  15.5 21.8 %all-to-all-start = ((bf16[5,8,4096]{2,0,1:T(8,128)(2,1)}), bf16[5,8,4096]{2,0,1:T(8,128)(2,1)S(1)}, u32[]{:S(2)}, u32[]{:S(2)}) async-start(bf16[5,8,4096]{2,0,1:T(8,128)(2,1)} %copy.18), calls=%async_computation | async-start | bytes 1048576 | tf_op jit(solution)/shard_map/all_to_all | solution.py:29
  22.8 89.9 %all-gather.4.cloned.1.call-start = ((), (), s32[]{:S(2)}) async-start(), calls=%async_computation.3 | async-start | bytes 1769472 | tf_op jit(solution)/shard_map/all_gather | solution.py:39
  39.7 274.2 %reduce-scatter.2.cloned.1.call-start = ((), (), s32[]{:S(2)}) async-start(), calls=%async_computation.4 | async-start | bytes 3538944 | tf_op jit(solution)/shard_map/reduce_scatter | solution.py:70
  220.9 93.8 %copy-start.3 = (s32[8]{0:T(128)S(1)}, s32[8]{0:T(128)}, u32[]{:S(2)}) copy-start(s32[8]{0:T(128)} %param.7) | copy-start | bytes 100
  239.2 95.0 %all-gather.6.cloned.1.call-start = ((), (), s32[]{:S(2)}) async-start(), calls=%async_computation.5 | async-start | bytes 1966080 | tf_op jit(solution)/shard_map/all_gather | solution.py:11
  337.4 24.7 %all-to-all-start.1 = ((bf16[5,8,1024]{2,0,1:T(8,128)(2,1)}), bf16[5,8,1024]{2,0,1:T(8,128)(2,1)S(1)}, u32[]{:S(2)}, u32[]{:S(2)}) async-start(bf16[5,8,1024]{2,0,1:T(8,128)(2,1)} %fusion.6), calls=%async_computation.2 | async-start | bytes 262144 | tf_op jit(solution)/shard_map/all_to_all | solution.py:87
Sparse Core Ops, SparseCore 0:
  39.8 43.2 all-gather.3
  239.3 74.4 reduce-scatter.1
  315.4 18.7 all-gather.5
